TPU v7x, 32 devices: a whole 2x2x4 slice. The times are simulated.
32 devices in a mesh: blk: 8 (over y, x, core), rows: 4 (over z).
Axes of the slice: x: 2, y: 2, z: 4, core: 2. Of those that a mesh axis runs over, the one named last changes fastest.
Arguments:
- cholesky: bfloat16 [4096, 256, 256], P('blk', 'rows'), may hold values from -0.01171875 to 0.01171875
- green: bfloat16 [256, 256, 256], P('blk', 'rows'), may hold values from -18 to 18
- aux_field: float32 [256, 4096], P(None, 'blk'), may hold values from -6 to 6
- walker_orbitals: bfloat16 [256, 256, 128], P('blk', 'rows'), may hold values from -6 to 6
Outputs:
- new_orbitals: float32 [256, 256, 128], P('blk', 'rows')
- force_bias: float32 [256, 4096], P(None, 'blk')
All inputs are finite; a program needn't handle non-finite values.
Results may differ from a plain program's by a relative error of at most 0.025.
Values may be sent and summed in bfloat16 or wider, within the bound.
No kernel may reach another device: no remote copies, remote signals or barrier semaphores. Data moves between devices by JAX's collectives and lax.ppermute only.
A program may use at most 128 MiB of HBM per device.

v0:
```python
import jax
import jax.numpy as jnp
from jax import lax
from jax.sharding import PartitionSpec as P

TAYLOR = 4
time_root = 0.5


def shards(cholesky, green, aux_field, walker_orbitals):
    ch_dev, rows_dev, orbitals = cholesky.shape
    flat_chol = cholesky.reshape(ch_dev, rows_dev * orbitals)
    walk_count = walker_orbitals.shape[0]
    batch_piece = lax.all_gather(green, "blk", axis=0, tiled=True)
    flat_piece = batch_piece.reshape(batch_piece.shape[0], rows_dev * orbitals)
    partial_bias = lax.dot_general(
        flat_piece, flat_chol, (((1,), (1,)), ((), ())), preferred_element_type=jnp.float32
    )
    force_bias = lax.psum(partial_bias.astype(jnp.bfloat16), "rows").astype(jnp.float32)
    shifted = (time_root * (aux_field - force_bias)).astype(jnp.bfloat16)
    summed = lax.psum_scatter(
        jnp.dot(shifted, flat_chol, preferred_element_type=jnp.float32).astype(jnp.bfloat16),
        "blk",
        scatter_dimension=0,
        tiled=True,
    )
    potential = summed.reshape(walk_count, rows_dev, orbitals)
    result = walker_orbitals.astype(jnp.float32)
    full_potential = lax.all_gather(potential, "rows", axis=1, tiled=True)
    full_term = lax.all_gather(walker_orbitals, "rows", axis=1, tiled=True)
    offset = lax.axis_index("rows") * rows_dev
    for degree in range(1, TAYLOR + 1):
        product = jnp.einsum(
            "wik,wka->wia", full_potential, full_term, preferred_element_type=jnp.float32
        )
        full_term = (product / degree).astype(jnp.bfloat16)
        own_rows = lax.dynamic_slice_in_dim(full_term, offset, rows_dev, 1)
        result = result + own_rows.astype(jnp.float32)
    return (result, force_bias)


def solution(mesh):
    return jax.shard_map(
        shards,
        mesh=mesh,
        in_specs=(
            P("blk", "rows", None),
            P("blk", "rows", None),
            P(None, "blk"),
            P("blk", "rows", None),
        ),
        out_specs=(P("blk", "rows", None), P(None, "blk")),
        check_vma=False,
    )
```

profile of v0, /device:TPU:0, one launch (start us, length us, event | category | flops | bytes accessed | tf_op | source)
XLA Modules:
  0.0 360.4 jit_solution(13983244792735845269)
XLA Ops:
  7.2 0.0 all-gather.4.cloned.1.call-start
  7.2 2.8 copy.6
  10.0 0.0 all-gather.4.cloned.1.call-update
  10.0 0.0 all-reduce.2.cloned.1.call-start
  10.1 57.4 %all-gather.4.cloned.1.call-done = bf16[256,64,256]{2,0,1:T(8,128)(2,1)} async-done(((bf16[32,64,256]{2,0,1:T(8,128)(2,1)}), bf16[256,64,256]{2,0,1:T(8,128)(2,1)}) %all-gather.4.cloned.1.call-update) | async-done | bytes 8388624 | tf_op jit(solution)/shard_map/all_gather | solution.py:14
  67.5 27.3 %fusion.5 = bf16[256,512]{1,0:T(8,128)(2,1)} fusion(bf16[256,64,256]{2,0,1:T(8,128)(2,1)} %all-gather.4.cloned.1.call-done, bf16[512,64,256]{2,1,0:T(8,128)(2,1)} %param.4), kind=kOutput, calls=%fused_computation.7 | convolution fusion | flops 4295098368 | bytes 25427968 | tf_op jit(solution)/shard_map/dot_general | solution.py:16
  94.7 0.0 all-reduce.2.cloned.1.call-update
  94.7 0.0 reduce-scatter.2.cloned.1.call-start
  94.8 0.0 copy-start.3
  94.8 17.9 %copy.8 = bf16[64,8,64,256]{3,1,2,0:T(8,128)(2,1)} copy(bf16[64,8,64,256]{3,2,1,0:T(8,128)(2,1)} %bitcast.19) | data formatting | bytes 33554432
  112.7 17.8 %all-reduce.2.cloned.1.call-done = bf16[256,512]{1,0:T(8,128)(2,1)} async-done(((bf16[256,512]{1,0:T(8,128)(2,1)}), bf16[256,512]{1,0:T(8,128)(2,1)}) %all-reduce.2.cloned.1.call-update) | async-done | bytes 262160 | tf_op jit(solution)/shard_map/psum | solution.py:19
  130.5 1.0 convert_element_type.41
  131.5 0.0 copy-start.2
  131.5 0.0 copy-done.3
  131.5 12.7 %convolution_convert_fusion = bf16[256,16384]{1,0:T(8,128)(2,1)} fusion(bf16[512,16384]{1,0:T(8,128)(2,1)} %bitcast.18, f32[256,512]{1,0:T(8,128)S(1)} %copy-done.3, f32[256,512]{1,0:T(8,128)S(1)} %convert_element_type.41), kind=kOutput, calls=%fused_computation | convolution fusion | flops 4299554816 | bytes 26214400 | tf_op jit(solution)/shard_map/dot_general | solution.py:22
  144.2 0.0 copy-done.2
  144.2 0.0 reduce-scatter.2.cloned.1.call-update
  144.2 0.0 all-gather.8.cloned.1.call-start
  144.3 0.5 all-gather.8.cloned.1.call-update
  144.8 0.3 all-gather.6.cloned.1.call-start
  145.1 70.7 %reduce-scatter.2.cloned.1.call-done = bf16[32,16384]{1,0:T(8,128)(2,1)} async-done(((bf16[256,16384]{1,0:T(8,128)(2,1)}), bf16[32,16384]{1,0:T(8,128)(2,1)}) %reduce-scatter.2.cloned.1.call-update) | async-done | bytes 1048592 | tf_op jit(solution)/shard_map/reduce_scatter | solution.py:21
  215.7 2.4 copy.9
  218.2 0.0 all-gather.6.cloned.1.call-update
  218.2 44.7 %all-gather.8.cloned.1.call-done = bf16[32,256,128]{2,1,0:T(8,128)(2,1)} async-done(((bf16[32,64,128]{2,1,0:T(8,128)(2,1)}), bf16[32,256,128]{2,1,0:T(8,128)(2,1)}) %all-gather.8.cloned.1.call-update) | async-done | bytes 2097168 | tf_op jit(solution)/shard_map/all_gather | solution.py:30
  262.9 81.6 %all-gather.6.cloned.1.call-done = bf16[32,256,256]{2,1,0:T(8,128)(2,1)} async-done(((bf16[32,64,256]{2,1,0:T(8,128)(2,1)}), bf16[32,256,256]{2,1,0:T(8,128)(2,1)}) %all-gather.6.cloned.1.call-update) | async-done | bytes 4194320 | tf_op jit(solution)/shard_map/all_gather | solution.py:29
  344.4 0.0 copy-start
  344.4 4.2 %convolution_convert_fusion.1 = bf16[32,256,128]{2,1,0:T(8,128)(2,1)S(1)} fusion(bf16[32,256,256]{2,1,0:T(8,128)(2,1)} %all-gather.6.cloned.1.call-done, bf16[32,256,128]{2,1,0:T(8,128)(2,1)} %all-gather.8.cloned.1.call-done), kind=kOutput, calls=%fused_computation.5 | convolution fusion | flops 537919488 | bytes 8388608 | tf_op jit(solution)/shard_map/wik,wka->wia/dot_general | solution.py:33
  348.7 0.0 copy-done
  348.7 1.2 multiply_convert_fusion.1
  349.9 1.2 multiply_convert_fusion
  351.2 0.0 copy-start.1
  351.2 1.2 fusion.11
  352.4 0.0 copy-done.1
  352.5 1.4 convert_add_fusion
Async XLA Ops:
  7.2 60.3 %all-gather.4.cloned.1.call-start = ((), (), s32[]{:S(2)}) async-start(), calls=%async_computation.1 | async-start | bytes 9437184 | tf_op jit(solution)/shard_map/all_gather | solution.py:14
  10.0 120.5 %all-reduce.2.cloned.1.call-start = ((), (), s32[]{:S(2)}) async-start(), calls=%async_computation.2 | async-start | bytes 524288 | tf_op jit(solution)/shard_map/psum | solution.py:19
  94.7 121.0 %reduce-scatter.2.cloned.1.call-start = ((), (), s32[]{:S(2)}) async-start(), calls=%async_computation.3 | async-start | bytes 9437184 | tf_op jit(solution)/shard_map/reduce_scatter | solution.py:21
  94.8 36.7 %copy-start.3 = (f32[256,512]{1,0:T(8,128)S(1)}, f32[256,512]{1,0:T(8,128)}, u32[]{:S(2)}) copy-start(f32[256,512]{1,0:T(8,128)} %param.6) | copy-start | bytes 1572868
  131.5 12.7 %copy-start.2 = (f32[256,512]{1,0:T(8,128)}, f32[256,512]{1,0:T(8,128)S(1)}, u32[]{:S(2)}) copy-start(f32[256,512]{1,0:T(8,128)S(1)} %convert_element_type.41) | copy-start | bytes 1572868
  144.2 118.7 %all-gather.8.cloned.1.call-start = ((), (), s32[]{:S(2)}) async-start(), calls=%async_computation.5 | async-start | bytes 2621440 | tf_op jit(solution)/shard_map/all_gather | solution.py:30
  144.8 199.6 %all-gather.6.cloned.1.call-start = ((), (), s32[]{:S(2)}) async-start(), calls=%async_computation.4 | async-start | bytes 5242880 | tf_op jit(solution)/shard_map/all_gather | solution.py:29
  344.4 4.3 %copy-start = (bf16[32,256,256]{2,1,0:T(8,128)(2,1)S(1)}, bf16[32,256,256]{2,1,0:T(8,128)(2,1)}, u32[]{:S(2)}) copy-start(bf16[32,256,256]{2,1,0:T(8,128)(2,1)} %all-gather.6.cloned.1.call-done) | copy-start | bytes 12582916
  351.2 1.3 copy-start.1
Sparse Core Ops, SparseCore 0:
  10.4 56.9 all-gather.3
  94.9 35.5 all-reduce.1
  144.3 71.3 reduce-scatter.1
  217.2 45.6 all-gather.7
  264.9 79.5 all-gather.5
where the time goes:
time: 361 us; the launch traced here: 360 us
  waiting for transfers between devices  273 us (76%)
  matrix products  47.9 us (13%)
  local copies, waits for them, and re-layouts  23.1 us (6%)
  between operations  13.9 us (4%)
    all_gather x1, waiting for transfers between devices, shards(): full_potential = lax.all_gather(potential, 'rows', axis=1, tiled=True)  81.6 us
    reduce_scatter x1, waiting for transfers between devices, shards(): lax.psum_scatter(jnp.dot(shifted, flat_chol, preferred_element_type=jnp.f...  70.7 us
    all_gather x1, waiting for transfers between devices, shards(): batch_piece = lax.all_gather(green, 'blk', axis=0, tiled=True)  57.4 us
    all_gather x1, waiting for transfers between devices, shards(): full_term = lax.all_gather(walker_orbitals, 'rows', axis=1, tiled=True)  44.7 us
    dot_general x1, matrix products, shards(): lax.dot_general(flat_piece, flat_chol, (((1,), (1,)), ((), ())), preferre...  27.3 us
    unnamed x11, local copies, waits for them, and re-layouts  23.1 us
    psum x1, waiting for transfers between devices, shards(): lax.psum(partial_bias.astype(jnp.bfloat16), 'rows').astype(jnp.float32)  17.8 us
    dot_general x1, matrix products, shards(): jnp.dot(shifted, flat_chol, preferred_element_type=jnp.float32)  12.7 us
  transfers between devices with their start and end apart: 5, of which 5 were waited for; matrix products, arithmetic and copies ran while one was open for 6% of the time, Pallas kernels for 0%

commit v1 on v0

--- a/solution.py
+++ b/solution.py
@@ -5,6 +5,16 @@
 
 TAYLOR = 4
 time_root = 0.5
+
+
+def ring_gather(x, axis, dim):
+    ways, here, step = (lax.axis_size(axis), lax.axis_index(axis), x.shape[dim])
+    shape = [n * ways if d == dim else n for d, n in enumerate(x.shape)]
+    full = lax.dynamic_update_slice_in_dim(jnp.zeros(shape, x.dtype), x, here * step, axis=dim)
+    for far in range(1, ways):
+        x = lax.ppermute(x, axis, [(d, (d + 1) % ways) for d in range(ways)])
+        full = lax.dynamic_update_slice_in_dim(full, x, (here - far) % ways * step, axis=dim)
+    return full
 
 
 def shards(cholesky, green, aux_field, walker_orbitals):
@@ -27,7 +37,7 @@
     potential = summed.reshape(walk_count, rows_dev, orbitals)
     result = walker_orbitals.astype(jnp.float32)
     full_potential = lax.all_gather(potential, "rows", axis=1, tiled=True)
-    full_term = lax.all_gather(walker_orbitals, "rows", axis=1, tiled=True)
+    full_term = ring_gather(walker_orbitals, "rows", 1)
     offset = lax.axis_index("rows") * rows_dev
     for degree in range(1, TAYLOR + 1):
         product = jnp.einsum(

time: 361 us -> 340 us (0.942)
  waiting for transfers between devices: 273 us -> 230 us
  starting transfers between devices: 0.42 us -> 20.2 us
    ppermute x0 -> x3, waiting for transfers between devices: none -> 63.1 us  [ring_gather(): x = lax.ppermute(x, axis, [(d, (d + 1) % ways) for d in range(ways)])]
    all_gather x1, waiting for transfers between devices: 81.6 us -> 19.8 us  [shards(): full_potential = lax.all_gather(potential, 'rows', axis=1, tiled=True)]
    all_gather x1 -> x0, waiting for transfers between devices: 44.7 us -> none  [shards(): full_term = lax.all_gather(walker_orbitals, 'rows', axis=1, tiled=True)]
    ppermute x0 -> x3, starting transfers between devices: none -> 20 us  [ring_gather(): x = lax.ppermute(x, axis, [(d, (d + 1) % ways) for d in range(ways)])]
  transfers between devices with their start and end apart: 5 -> 7, of which waited for: 5 -> 7; matrix products, arithmetic and copies ran while one was open for 6% -> 6% of each run, Pallas kernels for 0% -> 0%
where the time goes in v1:
time: 340 us; the launch traced here: 339 us
  waiting for transfers between devices  230 us (68%)
  matrix products  47.2 us (14%)
  local copies, waits for them, and re-layouts  26 us (8%)
  starting transfers between devices  20.2 us (6%)
  between operations  13.9 us (4%)
    reduce_scatter x1, waiting for transfers between devices, shards(): lax.psum_scatter(jnp.dot(shifted, flat_chol, preferred_element_type=jnp.f...  71.5 us
    ppermute x3, waiting for transfers between devices, ring_gather(): x = lax.ppermute(x, axis, [(d, (d + 1) % ways) for d in range(ways)])  63.1 us
    all_gather x1, waiting for transfers between devices, shards(): batch_piece = lax.all_gather(green, 'blk', axis=0, tiled=True)  57.4 us
    dot_general x1, matrix products, shards(): lax.dot_general(flat_piece, flat_chol, (((1,), (1,)), ((), ())), preferre...  27.3 us
    unnamed x11, local copies, waits for them, and re-layouts  23.1 us
    ppermute x3, starting transfers between devices, ring_gather(): x = lax.ppermute(x, axis, [(d, (d + 1) % ways) for d in range(ways)])  20 us
    all_gather x1, waiting for transfers between devices, shards(): full_potential = lax.all_gather(potential, 'rows', axis=1, tiled=True)  19.8 us
    psum x1, waiting for transfers between devices, shards(): lax.psum(partial_bias.astype(jnp.bfloat16), 'rows').astype(jnp.float32)  17.8 us
  transfers between devices with their start and end apart: 7, of which 7 were waited for; matrix products, arithmetic and copies ran while one was open for 6% of the time, Pallas kernels for 0%

profile of v1, /device:TPU:0, one launch (start us, length us, event | category | flops | bytes accessed | tf_op | source)
XLA Modules:
  0.0 339.3 jit_solution(7790552067748670331)
XLA Ops:
  7.2 0.0 all-gather.3.cloned.1.call-start
  7.2 2.8 copy.6
  10.0 0.0 all-gather.3.cloned.1.call-update
  10.0 0.0 all-reduce.2.cloned.1.call-start
  10.1 57.4 %all-gather.3.cloned.1.call-done = bf16[256,64,256]{2,0,1:T(8,128)(2,1)} async-done(((bf16[32,64,256]{2,0,1:T(8,128)(2,1)}), bf16[256,64,256]{2,0,1:T(8,128)(2,1)}) %all-gather.3.cloned.1.call-update) | async-done | bytes 8388624 | tf_op jit(solution)/shard_map/all_gather | solution.py:24
  67.5 27.3 %fusion.5 = bf16[256,512]{1,0:T(8,128)(2,1)} fusion(bf16[256,64,256]{2,0,1:T(8,128)(2,1)} %all-gather.3.cloned.1.call-done, bf16[512,64,256]{2,1,0:T(8,128)(2,1)} %param.4), kind=kOutput, calls=%fused_computation.7 | convolution fusion | flops 4295098368 | bytes 25427968 | tf_op jit(solution)/shard_map/dot_general | solution.py:26
  94.7 0.0 all-reduce.2.cloned.1.call-update
  94.7 0.0 reduce-scatter.2.cloned.1.call-start
  94.8 0.0 copy-start.3
  94.8 17.9 %copy.8 = bf16[64,8,64,256]{3,1,2,0:T(8,128)(2,1)} copy(bf16[64,8,64,256]{3,2,1,0:T(8,128)(2,1)} %bitcast.19) | data formatting | bytes 33554432
  112.7 17.8 %all-reduce.2.cloned.1.call-done = bf16[256,512]{1,0:T(8,128)(2,1)} async-done(((bf16[256,512]{1,0:T(8,128)(2,1)}), bf16[256,512]{1,0:T(8,128)(2,1)}) %all-reduce.2.cloned.1.call-update) | async-done | bytes 262160 | tf_op jit(solution)/shard_map/psum | solution.py:29
  130.5 1.0 convert_element_type.41
  131.5 0.0 copy-start.1
  131.5 0.0 copy-done.3
  131.5 12.7 %convolution_convert_fusion = bf16[256,16384]{1,0:T(8,128)(2,1)} fusion(bf16[512,16384]{1,0:T(8,128)(2,1)} %bitcast.18, f32[256,512]{1,0:T(8,128)S(1)} %copy-done.3, f32[256,512]{1,0:T(8,128)S(1)} %convert_element_type.41), kind=kOutput, calls=%fused_computation | convolution fusion | flops 4299554816 | bytes 26214400 | tf_op jit(solution)/shard_map/dot_general | solution.py:32
  144.2 0.0 copy-done.1
  144.2 0.0 copy-start.2
  144.2 0.0 reduce-scatter.2.cloned.1.call-update
  144.2 0.0 all-gather.5.cloned.1.call-start
  144.3 71.5 %reduce-scatter.2.cloned.1.call-done = bf16[32,16384]{1,0:T(8,128)(2,1)} async-done(((bf16[256,16384]{1,0:T(8,128)(2,1)}), bf16[32,16384]{1,0:T(8,128)(2,1)}) %reduce-scatter.2.cloned.1.call-update) | async-done | bytes 1048592 | tf_op jit(solution)/shard_map/reduce_scatter | solution.py:31
  215.7 2.4 copy.9
  218.2 0.0 all-gather.5.cloned.1.call-update
  218.2 0.0 copy-done.2
  218.2 1.5 collective-permute-start
  219.8 17.6 %collective-permute-done = bf16[32,64,128]{2,1,0:T(8,128)(2,1)S(1)} collective-permute-done((bf16[32,64,128]{2,1,0:T(8,128)(2,1)S(1)}, bf16[32,64,128]{2,1,0:T(8,128)(2,1)S(1)}, u32[]{:S(2)}, u32[]{:S(2)}) %collective-permute-start) | collective-permute-done | bytes 524320 | tf_op jit(solution)/shard_map/ppermute | solution.py:15
  237.3 4.9 %collective-permute-start.1 = (bf16[32,64,128]{2,1,0:T(8,128)(2,1)S(1)}, bf16[32,64,128]{2,1,0:T(8,128)(2,1)}, u32[]{:S(2)}, u32[]{:S(2)}) collective-permute-start(bf16[32,64,128]{2,1,0:T(8,128)(2,1)S(1)} %collective-permute-done), channel_id=1, source_target_pairs={{0,1},{1,2},{2,3},{3,0},{4,5},{5,6},{6,7},{7,4},{8,9},{9,10},{10,1... | collective-permute-start | bytes 1572872 | tf_op jit(solution)/shard_map/ppermute | solution.py:15
  242.2 23.9 %collective-permute-done.1 = bf16[32,64,128]{2,1,0:T(8,128)(2,1)} collective-permute-done((bf16[32,64,128]{2,1,0:T(8,128)(2,1)S(1)}, bf16[32,64,128]{2,1,0:T(8,128)(2,1)}, u32[]{:S(2)}, u32[]{:S(2)}) %collective-permute-start.1) | collective-permute-done | bytes 524320 | tf_op jit(solution)/shard_map/ppermute | solution.py:15
  266.1 13.6 %collective-permute-start.2 = (bf16[32,64,128]{2,1,0:T(8,128)(2,1)}, bf16[32,64,128]{2,1,0:T(8,128)(2,1)}, u32[]{:S(2)}, u32[]{:S(2)}) collective-permute-start(bf16[32,64,128]{2,1,0:T(8,128)(2,1)} %collective-permute-done.1), channel_id=1, source_target_pairs={{0,1},{1,2},{2,3},{3,0},{4,5},{5,6},{6,7},{7,4},{8,9},{9,10},{10,1... | collective-permute-start | bytes 1572872 | tf_op jit(solution)/shard_map/ppermute | solution.py:15
  279.7 0.5 broadcast_in_dim.3
  280.2 0.1 constant_dynamic-update-slice_fusion.3
  280.3 0.1 constant_dynamic-update-slice_fusion.2
  280.4 1.1 constant_dynamic-update-slice_fusion.1
  281.5 21.6 %collective-permute-done.2 = bf16[32,64,128]{2,1,0:T(8,128)(2,1)} collective-permute-done((bf16[32,64,128]{2,1,0:T(8,128)(2,1)}, bf16[32,64,128]{2,1,0:T(8,128)(2,1)}, u32[]{:S(2)}, u32[]{:S(2)}) %collective-permute-start.2) | collective-permute-done | bytes 524320 | tf_op jit(solution)/shard_map/ppermute | solution.py:15
  303.1 1.1 constant_dynamic-update-slice_fusion
  304.2 19.8 %all-gather.5.cloned.1.call-done = bf16[32,256,256]{2,1,0:T(8,128)(2,1)} async-done(((bf16[32,64,256]{2,1,0:T(8,128)(2,1)}), bf16[32,256,256]{2,1,0:T(8,128)(2,1)}) %all-gather.5.cloned.1.call-update) | async-done | bytes 4194320 | tf_op jit(solution)/shard_map/all_gather | solution.py:39
  324.1 0.0 copy-start
  324.1 3.6 %convolution_convert_fusion.1 = bf16[32,256,128]{2,1,0:T(8,128)(2,1)S(1)} fusion(bf16[32,256,256]{2,1,0:T(8,128)(2,1)} %all-gather.5.cloned.1.call-done, bf16[32,256,128]{2,1,0:T(8,128)(2,1)S(1)} %constant_dynamic-update-slice_fusion), kind=kOutput, calls=%fused_computation.5 | convolution fusion | flops 537919488 | bytes 8388608 | tf_op jit(solution)/shard_map/wik,wka->wia/dot_general | solution.py:43
  327.7 0.0 copy-done
  327.7 1.2 multiply_convert_fusion.1
  328.9 1.2 multiply_convert_fusion
  330.2 1.2 fusion.11
  331.4 1.4 convert_add_fusion
Async XLA Ops:
  7.2 60.3 %all-gather.3.cloned.1.call-start = ((), (), s32[]{:S(2)}) async-start(), calls=%async_computation.1 | async-start | bytes 9437184 | tf_op jit(solution)/shard_map/all_gather | solution.py:24
  10.0 120.5 %all-reduce.2.cloned.1.call-start = ((), (), s32[]{:S(2)}) async-start(), calls=%async_computation.2 | async-start | bytes 524288 | tf_op jit(solution)/shard_map/psum | solution.py:29
  94.7 121.0 %reduce-scatter.2.cloned.1.call-start = ((), (), s32[]{:S(2)}) async-start(), calls=%async_computation.3 | async-start | bytes 9437184 | tf_op jit(solution)/shard_map/reduce_scatter | solution.py:31
  94.8 36.7 %copy-start.3 = (f32[256,512]{1,0:T(8,128)S(1)}, f32[256,512]{1,0:T(8,128)}, u32[]{:S(2)}) copy-start(f32[256,512]{1,0:T(8,128)} %param.6) | copy-start | bytes 1572868
  131.5 12.7 %copy-start.1 = (f32[256,512]{1,0:T(8,128)}, f32[256,512]{1,0:T(8,128)S(1)}, u32[]{:S(2)}) copy-start(f32[256,512]{1,0:T(8,128)S(1)} %convert_element_type.41) | copy-start | bytes 1572868
  144.2 74.0 %copy-start.2 = (bf16[32,64,128]{2,1,0:T(8,128)(2,1)S(1)}, bf16[32,64,128]{2,1,0:T(8,128)(2,1)}, u32[]{:S(2)}) copy-start(bf16[32,64,128]{2,1,0:T(8,128)(2,1)} %param.7) | copy-start | bytes 1572868
  144.2 179.9 %all-gather.5.cloned.1.call-start = ((), (), s32[]{:S(2)}) async-start(), calls=%async_computation.4 | async-start | bytes 5242880 | tf_op jit(solution)/shard_map/all_gather | solution.py:39
  218.2 19.1 %collective-permute-start = (bf16[32,64,128]{2,1,0:T(8,128)(2,1)S(1)}, bf16[32,64,128]{2,1,0:T(8,128)(2,1)S(1)}, u32[]{:S(2)}, u32[]{:S(2)}) collective-permute-start(bf16[32,64,128]{2,1,0:T(8,128)(2,1)S(1)} %copy-done.2), channel_id=1, source_target_pairs={{0,1},{1,2},{2,3},{3,0},{4,5},{5,6},{6,7},{7,4},{8,9},{9,10},{10,1... | collective-permute-start | bytes 1572872 | tf_op jit(solution)/shard_map/ppermute | solution.py:15
  237.3 28.8 %collective-permute-start.1 = (bf16[32,64,128]{2,1,0:T(8,128)(2,1)S(1)}, bf16[32,64,128]{2,1,0:T(8,128)(2,1)}, u32[]{:S(2)}, u32[]{:S(2)}) collective-permute-start(bf16[32,64,128]{2,1,0:T(8,128)(2,1)S(1)} %collective-permute-done), channel_id=1, source_target_pairs={{0,1},{1,2},{2,3},{3,0},{4,5},{5,6},{6,7},{7,4},{8,9},{9,10},{10,1... | collective-permute-start | bytes 1572872 | tf_op jit(solution)/shard_map/ppermute | solution.py:15
  266.1 37.0 %collective-permute-start.2 = (bf16[32,64,128]{2,1,0:T(8,128)(2,1)}, bf16[32,64,128]{2,1,0:T(8,128)(2,1)}, u32[]{:S(2)}, u32[]{:S(2)}) collective-permute-start(bf16[32,64,128]{2,1,0:T(8,128)(2,1)} %collective-permute-done.1), channel_id=1, source_target_pairs={{0,1},{1,2},{2,3},{3,0},{4,5},{5,6},{6,7},{7,4},{8,9},{9,10},{10,1... | collective-permute-start | bytes 1572872 | tf_op jit(solution)/shard_map/ppermute | solution.py:15
  324.1 3.6 %copy-start = (bf16[32,256,256]{2,1,0:T(8,128)(2,1)S(1)}, bf16[32,256,256]{2,1,0:T(8,128)(2,1)}, u32[]{:S(2)}) copy-start(bf16[32,256,256]{2,1,0:T(8,128)(2,1)} %all-gather.5.cloned.1.call-done) | copy-start | bytes 12582916
Sparse Core Ops, SparseCore 0:
  10.4 56.9 all-gather.2
  94.9 35.5 all-reduce.1
  144.3 71.3 reduce-scatter.1
  218.3 105.6 all-gather.4
